TPU v7x, 32 devices: a whole 2x2x4 slice. The times are simulated.
32 devices in a mesh: verts: 8 (over z, y), modes: 4 (over x, core).
Axes of the slice: x: 2, y: 2, z: 4, core: 2. Of those that a mesh axis runs over, the one named last changes fastest.
Arguments:
- reduced_coords: float32 [256], P('modes'), may hold values from -4 to 4
- mode_basis: bfloat16 [256, 3, 8192], P('modes', None, 'verts'), may hold values from -0.375 to 0.375
- rest_shape: float32 [3, 8192], P(None, 'verts'), may hold values from -6 to 6
- stiffness: float32 [8192], P('verts'), may hold values from 0.2 to 2
- send_slots: int32 [8, 8, 16], P('verts'), may hold values from 0 to 1023
- pair_peer: int32 [8, 2, 1024], P('verts'), may hold values from 0 to 7
- pair_slot: int32 [8, 2, 1024], P('verts'), may hold values from 0 to 15
- pair_count: int32 [8], P('verts'), may hold values from 1 to 1024, 4096 in all
Outputs:
- hessian: float32 [256, 256], P('modes')
- gradient: float32 [256], P('modes')
Inputs may be any that keep to these rules, and one draw needn't show every extreme that they name: `send_slots`: indices may repeat. `pair_count`: the counts sum to 8 * 512 and the busiest owner has all 1024 slots live; slots at and beyond an owner's count hold valid but unused indices.
All inputs are finite; a program needn't handle non-finite values. No bound on the sum of `pair_count` on one device may be relied on, other than what follows from the above.
Results may differ from a plain program's by a relative error of at most 0.0046.
Values may be sent and summed in bfloat16 or wider, within the bound.
No kernel may reach another device: no remote copies, remote signals or barrier semaphores. Data moves between devices by JAX's collectives and lax.ppermute only.
A program may use at most 64 MiB of HBM per device.

v0:
```python
import jax
import jax.numpy as jnp
from jax import lax
from jax.sharding import PartitionSpec as P

highest = lax.Precision.HIGHEST
barrier_reach = 1.5
gap_offset = 0.1


def barrier_slopes(distance):
    excess = distance - barrier_reach
    ratio_log = jnp.log(distance / barrier_reach)
    slope_term = -(2.0 * excess * ratio_log + excess * excess / distance)
    curvature = -(
        2.0 * ratio_log + 4.0 * excess / distance - excess * excess / (distance * distance)
    )
    inside = distance < barrier_reach
    return (jnp.where(inside, slope_term, 0.0), jnp.where(inside, curvature, 0.0))


def outer_sum(left_rows, right_rows):
    return lax.dot_general(
        left_rows, right_rows, (((1,), (1,)), ((), ())), preferred_element_type=jnp.float32
    )


def spring_terms(displacement, stiffness):
    radius = jnp.sqrt(1.0 + jnp.sum(displacement * displacement, axis=0))
    spring_rate = stiffness / radius
    return (spring_rate, -spring_rate / (radius * radius), spring_rate * displacement)


def elastic_left(basis_block, displacement, spring_rate, curvature_rate):
    mode_count, _, vertex_count = basis_block.shape
    projected = jnp.sum(basis_block * displacement[None], axis=1)
    scaled = (spring_rate * basis_block).astype(jnp.bfloat16)
    return jnp.concatenate(
        [
            scaled.reshape(mode_count, 3 * vertex_count),
            (curvature_rate * projected).astype(jnp.bfloat16),
        ],
        axis=1,
    )


def elastic_right(basis_block, displacement):
    mode_count, _, vertex_count = basis_block.shape
    projected = jnp.sum(basis_block * displacement[None], axis=1)
    return jnp.concatenate(
        [basis_block.reshape(mode_count, 3 * vertex_count), projected.astype(jnp.bfloat16)], axis=1
    )


def contact_terms(rows_first, rows_second, separation, active):
    mode_count, _, slot_total = rows_first.shape
    distance = jnp.sum(separation * separation, axis=0) + gap_offset
    slope_term, curvature = barrier_slopes(distance)
    slope_term = slope_term * active
    curvature = curvature * active
    difference = rows_first.astype(jnp.float32) - rows_second.astype(jnp.float32)
    leverage = jnp.sum(difference * separation[None], axis=1)
    left_rows = jnp.concatenate(
        [
            (2.0 * slope_term * difference)
            .astype(jnp.bfloat16)
            .reshape(mode_count, 3 * slot_total),
            (4.0 * curvature * leverage).astype(jnp.bfloat16),
        ],
        axis=1,
    )
    right_rows = jnp.concatenate(
        [
            difference.astype(jnp.bfloat16).reshape(mode_count, 3 * slot_total),
            leverage.astype(jnp.bfloat16),
        ],
        axis=1,
    )
    contact_grad = jnp.sum(difference * (2.0 * slope_term * separation)[None], axis=(1, 2))
    return (left_rows, right_rows, contact_grad)


def body(
    reduced_coords, mode_basis, rest_shape, stiffness, send_slots, pair_peer, pair_slot, pair_count
):
    local_modes, _, vertex_count = mode_basis.shape
    peer_count = lax.axis_size("verts")
    mode_groups = lax.axis_size("modes")
    mode_count = local_modes * mode_groups
    factor = mode_count / (3.0 * vertex_count * peer_count)
    partial_value = jnp.dot(
        reduced_coords,
        mode_basis.reshape(local_modes, 3 * vertex_count),
        precision=highest,
        preferred_element_type=jnp.float32,
    ).reshape(3, vertex_count)
    positions = rest_shape + lax.psum(partial_value, "modes")
    displacement = positions - rest_shape
    spring_rate, curvature_rate, elastic_force = spring_terms(displacement, stiffness)
    send_ids = send_slots[0]
    slot_count = send_ids.shape[1]
    flat_slots = send_ids.reshape(-1)
    outgoing_pos = jnp.take(positions, flat_slots, axis=1).reshape(3, peer_count, slot_count)
    outgoing_rows = jnp.take(mode_basis, flat_slots, axis=2).reshape(
        local_modes, 3, peer_count, slot_count
    )
    incoming_pos = lax.all_to_all(outgoing_pos, "verts", split_axis=1, concat_axis=1, tiled=True)
    incoming_rows = lax.all_to_all(outgoing_rows, "verts", split_axis=2, concat_axis=2, tiled=True)
    slot_total = pair_peer.shape[2]
    endpoints = (pair_peer[0] * slot_count + pair_slot[0]).reshape(-1)
    pos_ends = jnp.take(
        incoming_pos.reshape(3, peer_count * slot_count), endpoints, axis=1
    ).reshape(3, 2, slot_total)
    row_ends = jnp.take(
        incoming_rows.reshape(local_modes, 3, peer_count * slot_count), endpoints, axis=2
    ).reshape(local_modes, 3, 2, slot_total)
    separation = pos_ends[:, 0] - pos_ends[:, 1]
    active = (jnp.arange(slot_total, dtype=jnp.int32) < pair_count[0]).astype(jnp.float32)
    contact_left, contact_right, contact_grad = contact_terms(
        row_ends[:, :, 0], row_ends[:, :, 1], separation, active
    )
    left_rows = elastic_left(mode_basis, displacement, spring_rate, curvature_rate)
    hessian = outer_sum(
        left_rows,
        elastic_right(lax.all_gather(mode_basis, "modes", axis=0, tiled=True), displacement),
    )
    hessian = hessian + outer_sum(
        contact_left, lax.all_gather(contact_right, "modes", axis=0, tiled=True)
    )
    elastic_grad = jnp.dot(
        mode_basis.reshape(local_modes, 3 * vertex_count),
        elastic_force.reshape(3 * vertex_count),
        precision=highest,
        preferred_element_type=jnp.float32,
    )
    hessian, gradient = lax.psum((hessian, elastic_grad + contact_grad), "verts")
    return (hessian * factor, gradient * factor)


def solution(mesh):
    return jax.shard_map(
        body,
        mesh=mesh,
        in_specs=(
            P("modes"),
            P("modes", None, "verts"),
            P(None, "verts"),
            P("verts"),
            P("verts", None, None),
            P("verts", None, None),
            P("verts", None, None),
            P("verts"),
        ),
        out_specs=(P("modes", None), P("modes")),
        check_vma=False,
    )
```

profile of v0, /device:TPU:0, one launch (start us, length us, event | category | flops | bytes accessed | tf_op | source)
XLA Modules:
  0.0 166.1 jit_solution(15953994613902127670)
XLA Ops:
  7.2 0.0 all-gather.3.cloned.1.call-start
  7.2 0.7 all-gather.3.cloned.1.call-update
  7.9 0.8 reshape_squeeze.6
  8.7 0.7 compare_and_fusion.1
  9.4 1.3 fusion.20
  10.7 12.8 %psum.21 = f32[3,1024]{1,0:T(4,128)S(1)} all-reduce(f32[3,1024]{1,0:T(4,128)S(1)} %bitcast.91), channel_id=1, replica_groups=mesh['verts'=8,'modes'=4] {'modes'}, use_global_device_ids=true, to_apply=%region_0.0 | all-reduce | flops 3072 | bytes 24576 | tf_op jit(solution)/shard_map/psum | solution.py:97
  23.4 0.7 multiply_reduce_fusion.2
  24.2 0.2 copy.65
  24.4 0.6 gather_fusion
  25.1 0.1 copy.66
  25.2 0.6 broadcast_select_fusion.3
  25.8 5.9 %all-to-all-start = ((f32[3,8,16]{2,0,1:T(4,128)}), f32[3,8,16]{2,0,1:T(4,128)S(1)}, u32[]{:S(2)}, u32[]{:S(2)}) async-start(f32[3,8,16]{2,0,1:T(4,128)} %broadcast_select_fusion.3), calls=%async_computation | async-start | bytes 32768 | tf_op jit(solution)/shard_map/all_to_all | solution.py:107
  31.7 0.7 fusion.28
  32.4 0.7 compare_and_fusion
  33.2 0.7 copy.69
  33.9 0.7 gather_fusion.2
  34.7 0.1 copy_bitcast_fusion.2
  35.4 0.7 reshape.268
  36.2 2.1 %all-to-all-done = f32[3,8,16]{2,0,1:T(4,128)S(1)} async-done(((f32[3,8,16]{2,0,1:T(4,128)}), f32[3,8,16]{2,0,1:T(4,128)S(1)}, u32[]{:S(2)}, u32[]{:S(2)}) %all-to-all-start) | async-done | bytes 1568 | tf_op jit(solution)/shard_map/all_to_all | solution.py:107
  38.3 3.9 %all-to-all-start.1 = ((bf16[8,2,1536]{2,1,0:T(2,128)(2,1)}), bf16[8,2,1536]{2,1,0:T(2,128)(2,1)S(1)}, u32[]{:S(2)}, u32[]{:S(2)}) async-start(bf16[8,2,1536]{2,1,0:T(2,128)(2,1)} %reshape.268), calls=%async_computation.1 | async-start | bytes 98304 | tf_op jit(solution)/shard_map/all_to_all | solution.py:108
  42.2 0.1 copy.67
  42.4 5.5 %gather_fusion.1 = f32[2048,3]{1,0:T(8,128)S(1)} fusion(f32[3,128]{0,1:T(8,128)S(1)} %bitcast.82, s32[2048]{0:T(1024)S(1)} %broadcast_clamp_fusion), kind=kCustom, calls=%fused_computation.1 | custom fusion | bytes 57344 | tf_op jit(solution)/shard_map/jit(_take)/gather | solution.py:111
  47.8 0.3 copy.68
  48.2 0.7 all-to-all-done.1
  49.0 0.1 reshape.269
  49.1 0.1 copy.73
  49.2 6.9 %gather_fusion.3 = bf16[2048,64,3]{1,2,0:T(4,128)(2,1)S(1)} fusion(bf16[64,3,128]{0,1,2:T(4,128)(2,1)S(1)} %copy.73, s32[2048]{0:T(1024)S(1)} %broadcast_clamp_fusion), kind=kCustom, calls=%fused_computation.3 | custom fusion | bytes 1581056 | tf_op jit(solution)/shard_map/jit(_take)/gather | solution.py:114
  56.1 1.6 copy.74
  57.7 0.5 broadcast_select_fusion
  58.1 0.3 convert_subtract_fusion
  58.4 0.5 copy.82
  59.0 1.4 fusion.9
  60.3 0.7 multiply_convert_fusion.1
  61.0 0.8 pad_maximum_fusion
  61.9 0.0 all-reduce.2.cloned.1.call-start
  62.0 0.1 fusion.19
  62.1 0.8 copy.80
  62.9 0.7 multiply_convert_fusion.2
  63.6 0.4 fusion.7
  64.0 21.1 %psum.23 = f32[64]{0:T(128)S(1)} all-reduce(f32[64]{0:T(128)S(1)} %fusion.7), channel_id=1, replica_groups=mesh['verts'=8,'modes'=4] {'verts'}, use_global_device_ids=true, to_apply=%region_8.9 | all-reduce | flops 64 | bytes 512 | tf_op jit(solution)/shard_map/psum | solution.py:136
  85.2 1.9 %multiply_reduce_fusion = bf16[256,1024]{1,0:T(8,128)(2,1)S(1)} fusion(bf16[256,3,1024]{2,0,1:T(8,128)(2,1)} %all-gather.3.cloned.1.call-done, f32[3,1024]{1,0:T(4,128)} %copy-done.6), kind=kLoop, calls=%fused_computation.4 | loop fusion | flops 2097152 | bytes 2109440 | tf_op jit(solution)/shard_map/reduce_sum | solution.py:49
  87.1 1.0 copy.64
  88.1 0.7 copy.63
  88.8 2.5 %fusion.15 = f32[64,256]{1,0:T(8,128)S(1)} fusion(bf16[256,4096]{1,0:T(8,128)(2,1)} %all-gather.5.cloned.1.call-done, bf16[64,1024]{1,0:T(8,128)(2,1)} %get-tuple-element.11, bf16[64,3072]{1,0:T(8,128)(2,1)S(1)} %multiply_convert_fusion), kind=kOutput, calls=%fused_computation.26 | convolution fusion | flops 135266304 | bytes 2686976 | tf_op jit(solution)/shard_map/dot_general | solution.py:23
  91.4 1.1 fusion.4
  92.5 0.5 broadcast_multiply_fusion.2
  93.0 65.1 %all-reduce.2.cloned.1.call-done = f32[64,256]{1,0:T(8,128)} async-done(((f32[64,256]{1,0:T(8,128)}), f32[64,256]{1,0:T(8,128)}) %all-reduce.2.cloned.1.call-update) | async-done | bytes 65552 | tf_op jit(solution)/shard_map/psum | solution.py:136
  158.1 1.5 broadcast_multiply_fusion
  (41 shorter events, 0.4 us)
Async XLA Ops:
  7.2 2.2 %copy-start = (f32[64]{0:T(128)S(1)}, f32[64]{0:T(128)}, u32[]{:S(2)}) copy-start(f32[64]{0:T(128)} %param.8) | copy-start | bytes 772
  7.2 26.0 %copy-start.2 = (bf16[64,3,1024]{2,0,1:T(8,128)(2,1)S(1)}, bf16[64,3,1024]{2,0,1:T(8,128)(2,1)}, u32[]{:S(2)}) copy-start(bf16[64,3,1024]{2,0,1:T(8,128)(2,1)} %param.9) | copy-start | bytes 1179652
  7.2 78.0 %all-gather.3.cloned.1.call-start = ((), (), s32[]{:S(2)}) async-start(), calls=%async_computation.2 | async-start | bytes 1966080 | tf_op jit(solution)/shard_map/all_gather | solution.py:125
  24.2 38.7 %copy-start.6 = (f32[3,1024]{1,0:T(4,128)}, f32[3,1024]{1,0:T(4,128)S(1)}, u32[]{:S(2)}) copy-start(f32[3,1024]{1,0:T(4,128)S(1)} %get-tuple-element.5) | copy-start | bytes 36868
  25.8 12.5 %all-to-all-start = ((f32[3,8,16]{2,0,1:T(4,128)}), f32[3,8,16]{2,0,1:T(4,128)S(1)}, u32[]{:S(2)}, u32[]{:S(2)}) async-start(f32[3,8,16]{2,0,1:T(4,128)} %broadcast_select_fusion.3), calls=%async_computation | async-start | bytes 32768 | tf_op jit(solution)/shard_map/all_to_all | solution.py:107
  38.3 10.7 %all-to-all-start.1 = ((bf16[8,2,1536]{2,1,0:T(2,128)(2,1)}), bf16[8,2,1536]{2,1,0:T(2,128)(2,1)S(1)}, u32[]{:S(2)}, u32[]{:S(2)}) async-start(bf16[8,2,1536]{2,1,0:T(2,128)(2,1)} %reshape.268), calls=%async_computation.1 | async-start | bytes 98304 | tf_op jit(solution)/shard_map/all_to_all | solution.py:108
  42.2 46.6 %all-gather.5.cloned.1.call-start = ((), (), s32[]{:S(2)}) async-start(), calls=%async_computation.3 | async-start | bytes 2621440 | tf_op jit(solution)/shard_map/all_gather | solution.py:128
  58.9 3.1 %copy-start.8 = (f32[1024]{0:T(1024)S(1)}, f32[1024]{0:T(1024)}, u32[]{:S(2)}) copy-start(f32[1024]{0:T(1024)} %param.11) | copy-start | bytes 12292
  58.9 3.1 %copy-start.3 = (bf16[64,3,1024]{2,0,1:T(8,128)(2,1)S(1)}, bf16[64,3,1024]{2,0,1:T(8,128)(2,1)}, u32[]{:S(2)}) copy-start(bf16[64,3,1024]{2,0,1:T(8,128)(2,1)} %param.9) | copy-start | bytes 1179652
  61.9 96.2 %all-reduce.2.cloned.1.call-start = ((), (), s32[]{:S(2)}) async-start(), calls=%async_computation.4 | async-start | bytes 131072 | tf_op jit(solution)/shard_map/psum | solution.py:136
  85.2 2.9 %copy-start.1 = (bf16[256,3,1024]{2,0,1:T(8,128)(2,1)S(1)}, bf16[256,3,1024]{2,0,1:T(8,128)(2,1)}, u32[]{:S(2)}) copy-start(bf16[256,3,1024]{2,0,1:T(8,128)(2,1)} %all-gather.3.cloned.1.call-done) | copy-start | bytes 4718596
  88.8 2.6 %copy-start.4 = (bf16[256,1024]{0,1:T(8,128)(2,1)S(1)}, bf16[256,1024]{0,1:T(8,128)(2,1)}, u32[]{:S(2)}) copy-start(bf16[256,1024]{0,1:T(8,128)(2,1)} %copy.64) | copy-start | bytes 1572868
  88.8 2.6 %copy-start.5 = (bf16[3,8,8,1024]{3,2,0,1:T(8,128)(2,1)S(1)}, bf16[3,8,8,1024]{3,2,0,1:T(8,128)(2,1)}, u32[]{:S(2)}) copy-start(bf16[3,8,8,1024]{3,2,0,1:T(8,128)(2,1)} %copy.80) | copy-start | bytes 1179652
  88.8 2.6 %copy-start.7 = (bf16[64,1024]{1,0:T(8,128)(2,1)S(1)}, bf16[64,1024]{1,0:T(8,128)(2,1)}, u32[]{:S(2)}) copy-start(bf16[64,1024]{1,0:T(8,128)(2,1)} %multiply_convert_fusion.2) | copy-start | bytes 393220
Sparse Core Ops, SparseCore 0:
  9.6 22.3 all-gather.2
  62.0 22.2 all-gather.4
  92.6 65.4 all-reduce.1
where the time goes:
time: 167 us; the launch traced here: 166 us
  waiting for transfers between devices  68.7 us (41%)
  blocking collectives  33.8 us (20%)
  local copies, waits for them, and re-layouts  21.5 us (13%)
  between operations  14.8 us (9%)
  other arithmetic  12.1 us (7%)
  starting transfers between devices  9.92 us (6%)
  matrix products  5.31 us (3%)
    psum x1, waiting for transfers between devices, body(): lax.psum((hessian, elastic_grad + contact_grad), 'verts')  65.1 us
    psum x1, blocking collectives, body(): lax.psum((hessian, elastic_grad + contact_grad), 'verts')  21.1 us
    psum x1, blocking collectives, body(): positions = rest_shape + lax.psum(partial_value, 'modes')  12.8 us
    gather x2, local copies, waits for them, and re-layouts, body(): jnp.take(incoming_rows.reshape(local_modes, 3, peer_count * slot_count),...  8.42 us
    all_to_all x1, starting transfers between devices, body(): lax.all_to_all(outgoing_pos, 'verts', split_axis=1, concat_axis=1, tiled=...  5.89 us
    gather x2, local copies, waits for them, and re-layouts, body(): jnp.take(incoming_pos.reshape(3, peer_count * slot_count), endpoints, axi...  5.79 us
    all_to_all x1, starting transfers between devices, body(): lax.all_to_all(outgoing_rows, 'verts', split_axis=2, concat_axis=2, tiled...  3.92 us
    dot_general x2, matrix products, outer_sum(): lax.dot_general(left_rows, right_rows, (((1,), (1,)), ((), ())), preferre...  3.62 us
  transfers between devices with their start and end apart: 5, of which 3 were waited for; matrix products, arithmetic and copies ran while one was open for 20% of the time, Pallas kernels for 0%

commit v1 on v0

--- a/solution.py
+++ b/solution.py
@@ -94,7 +94,7 @@
         precision=highest,
         preferred_element_type=jnp.float32,
     ).reshape(3, vertex_count)
-    positions = rest_shape + lax.psum(partial_value, "modes")
+    positions = rest_shape + jnp.sum(lax.all_gather(partial_value, "modes"), axis=0)
     displacement = positions - rest_shape
     spring_rate, curvature_rate, elastic_force = spring_terms(displacement, stiffness)
     send_ids = send_slots[0]

time: 167 us -> 162 us (0.970)
  blocking collectives: 33.8 us -> 27.3 us
    psum x1 -> x0, blocking collectives: 12.8 us -> none  [body(): positions = rest_shape + lax.psum(partial_value, 'modes')]
    all_gather x0 -> x1, blocking collectives: none -> 6.18 us  [body(): lax.all_gather(partial_value, 'modes')]
  transfers between devices with their start and end apart: 5 -> 5, of which waited for: 3 -> 3; matrix products, arithmetic and copies ran while one was open for 20% -> 21% of each run, Pallas kernels for 0% -> 0%
where the time goes in v1:
time: 162 us; the launch traced here: 161 us
  waiting for transfers between devices  69.7 us (43%)
  blocking collectives  27.3 us (17%)
  local copies, waits for them, and re-layouts  21.5 us (13%)
  between operations  14.8 us (9%)
  other arithmetic  12.1 us (7%)
  starting transfers between devices  10.4 us (6%)
  matrix products  5.31 us (3%)
    psum x1, waiting for transfers between devices, body(): lax.psum((hessian, elastic_grad + contact_grad), 'verts')  66.1 us
    psum x1, blocking collectives, body(): lax.psum((hessian, elastic_grad + contact_grad), 'verts')  21.1 us
    gather x2, local copies, waits for them, and re-layouts, body(): jnp.take(incoming_rows.reshape(local_modes, 3, peer_count * slot_count),...  8.42 us
    all_to_all x1, starting transfers between devices, body(): lax.all_to_all(outgoing_pos, 'verts', split_axis=1, concat_axis=1, tiled=...  6.36 us
    all_gather x1, blocking collectives, body(): lax.all_gather(partial_value, 'modes')  6.18 us
    gather x2, local copies, waits for them, and re-layouts, body(): jnp.take(incoming_pos.reshape(3, peer_count * slot_count), endpoints, axi...  5.79 us
    all_to_all x1, starting transfers between devices, body(): lax.all_to_all(outgoing_rows, 'verts', split_axis=2, concat_axis=2, tiled...  3.92 us
    dot_general x2, matrix products, outer_sum(): lax.dot_general(left_rows, right_rows, (((1,), (1,)), ((), ())), preferre...  3.61 us
  transfers between devices with their start and end apart: 5, of which 3 were waited for; matrix products, arithmetic and copies ran while one was open for 21% of the time, Pallas kernels for 0%

profile of v1, /device:TPU:0, one launch (start us, length us, event | category | flops | bytes accessed | tf_op | source)
XLA Modules:
  0.0 161.1 jit_solution(10486775143674730210)
XLA Ops:
  7.2 0.0 all-gather.5.cloned.1.call-start
  7.2 0.7 all-gather.5.cloned.1.call-update
  7.9 0.8 reshape_squeeze.6
  8.7 0.7 compare_and_fusion.1
  9.4 1.3 fusion.20
  10.7 6.2 %all-gather.1 = f32[4,3,1024]{2,1,0:T(4,128)S(1)} all-gather(f32[1,3,1024]{2,1,0:T(4,128)S(1)} %copy.77), channel_id=2, replica_groups=mesh['verts'=8,'modes'=4] {'modes'}, dimensions={0}, use_global_device_ids=true | all-gather | bytes 61440 | tf_op jit(solution)/shard_map/all_gather | solution.py:97
  16.9 0.7 multiply_reduce_fusion.2
  17.6 0.2 copy.66
  17.9 0.6 gather_fusion
  18.5 0.1 copy.67
  18.6 0.6 broadcast_select_fusion.3
  19.3 6.4 %all-to-all-start = ((f32[3,8,16]{2,0,1:T(4,128)}), f32[3,8,16]{2,0,1:T(4,128)S(1)}, u32[]{:S(2)}, u32[]{:S(2)}) async-start(f32[3,8,16]{2,0,1:T(4,128)} %broadcast_select_fusion.3), calls=%async_computation | async-start | bytes 32768 | tf_op jit(solution)/shard_map/all_to_all | solution.py:107
  25.6 0.7 fusion.28
  26.3 0.7 compare_and_fusion
  27.1 0.7 copy.70
  27.8 0.7 gather_fusion.2
  28.6 0.1 copy_bitcast_fusion.1
  29.4 0.7 reshape.277
  30.1 2.1 %all-to-all-done = f32[3,8,16]{2,0,1:T(4,128)S(1)} async-done(((f32[3,8,16]{2,0,1:T(4,128)}), f32[3,8,16]{2,0,1:T(4,128)S(1)}, u32[]{:S(2)}, u32[]{:S(2)}) %all-to-all-start) | async-done | bytes 1568 | tf_op jit(solution)/shard_map/all_to_all | solution.py:107
  32.2 3.9 %all-to-all-start.1 = ((bf16[8,2,1536]{2,1,0:T(2,128)(2,1)}), bf16[8,2,1536]{2,1,0:T(2,128)(2,1)S(1)}, u32[]{:S(2)}, u32[]{:S(2)}) async-start(bf16[8,2,1536]{2,1,0:T(2,128)(2,1)} %reshape.277), calls=%async_computation.1 | async-start | bytes 98304 | tf_op jit(solution)/shard_map/all_to_all | solution.py:108
  36.2 0.1 copy.68
  36.3 5.5 %gather_fusion.1 = f32[2048,3]{1,0:T(8,128)S(1)} fusion(f32[3,128]{0,1:T(8,128)S(1)} %bitcast.80, s32[2048]{0:T(1024)S(1)} %broadcast_clamp_fusion), kind=kCustom, calls=%fused_computation.1 | custom fusion | bytes 57344 | tf_op jit(solution)/shard_map/jit(_take)/gather | solution.py:111
  41.7 0.3 copy.69
  42.2 0.7 all-to-all-done.1
  42.9 0.1 reshape.278
  43.1 0.1 copy.74
  43.1 6.9 %gather_fusion.3 = bf16[2048,64,3]{1,2,0:T(4,128)(2,1)S(1)} fusion(bf16[64,3,128]{0,1,2:T(4,128)(2,1)S(1)} %copy.74, s32[2048]{0:T(1024)S(1)} %broadcast_clamp_fusion), kind=kCustom, calls=%fused_computation.3 | custom fusion | bytes 1581056 | tf_op jit(solution)/shard_map/jit(_take)/gather | solution.py:114
  50.0 1.6 copy.75
  51.6 0.5 broadcast_select_fusion
  52.0 0.3 convert_subtract_fusion
  52.3 0.5 copy.83
  52.9 1.4 fusion.9
  54.3 0.7 multiply_convert_fusion.1
  55.0 0.8 pad_maximum_fusion
  55.8 0.0 all-reduce.2.cloned.1.call-start
  55.9 0.1 fusion.19
  56.0 0.8 copy.81
  56.8 0.7 multiply_convert_fusion.2
  57.5 0.4 fusion.7
  58.0 21.1 %psum.15 = f32[64]{0:T(128)S(1)} all-reduce(f32[64]{0:T(128)S(1)} %fusion.7), channel_id=1, replica_groups=mesh['verts'=8,'modes'=4] {'verts'}, use_global_device_ids=true, to_apply=%region_8.9 | all-reduce | flops 64 | bytes 512 | tf_op jit(solution)/shard_map/psum | solution.py:136
  79.1 1.9 %multiply_reduce_fusion = bf16[256,1024]{1,0:T(8,128)(2,1)S(1)} fusion(bf16[256,3,1024]{2,0,1:T(8,128)(2,1)} %all-gather.5.cloned.1.call-done, f32[3,1024]{1,0:T(4,128)} %copy-done.6), kind=kLoop, calls=%fused_computation.4 | loop fusion | flops 2097152 | bytes 2109440 | tf_op jit(solution)/shard_map/reduce_sum | solution.py:49
  81.0 1.0 copy.65
  82.0 0.7 copy.64
  82.7 2.5 %fusion.15 = f32[64,256]{1,0:T(8,128)S(1)} fusion(bf16[256,4096]{1,0:T(8,128)(2,1)} %all-gather.7.cloned.1.call-done, bf16[64,1024]{1,0:T(8,128)(2,1)} %get-tuple-element.11, bf16[64,3072]{1,0:T(8,128)(2,1)S(1)} %multiply_convert_fusion), kind=kOutput, calls=%fused_computation.26 | convolution fusion | flops 135266304 | bytes 2686976 | tf_op jit(solution)/shard_map/dot_general | solution.py:23
  85.3 1.1 fusion.4
  86.4 0.5 broadcast_multiply_fusion.2
  86.9 66.1 %all-reduce.2.cloned.1.call-done = f32[64,256]{1,0:T(8,128)} async-done(((f32[64,256]{1,0:T(8,128)}), f32[64,256]{1,0:T(8,128)}) %all-reduce.2.cloned.1.call-update) | async-done | bytes 65552 | tf_op jit(solution)/shard_map/psum | solution.py:136
  153.1 1.5 broadcast_multiply_fusion
  (42 shorter events, 0.4 us)
Async XLA Ops:
  7.2 2.2 %copy-start = (f32[64]{0:T(128)S(1)}, f32[64]{0:T(128)}, u32[]{:S(2)}) copy-start(f32[64]{0:T(128)} %param.8) | copy-start | bytes 772
  7.2 19.9 %copy-start.2 = (bf16[64,3,1024]{2,0,1:T(8,128)(2,1)S(1)}, bf16[64,3,1024]{2,0,1:T(8,128)(2,1)}, u32[]{:S(2)}) copy-start(bf16[64,3,1024]{2,0,1:T(8,128)(2,1)} %param.9) | copy-start | bytes 1179652
  7.2 71.9 %all-gather.5.cloned.1.call-start = ((), (), s32[]{:S(2)}) async-start(), calls=%async_computation.2 | async-start | bytes 1966080 | tf_op jit(solution)/shard_map/all_gather | solution.py:125
  17.6 39.2 %copy-start.6 = (f32[3,1024]{1,0:T(4,128)}, f32[3,1024]{1,0:T(4,128)S(1)}, u32[]{:S(2)}) copy-start(f32[3,1024]{1,0:T(4,128)S(1)} %get-tuple-element.5) | copy-start | bytes 36868
  19.3 12.9 %all-to-all-start = ((f32[3,8,16]{2,0,1:T(4,128)}), f32[3,8,16]{2,0,1:T(4,128)S(1)}, u32[]{:S(2)}, u32[]{:S(2)}) async-start(f32[3,8,16]{2,0,1:T(4,128)} %broadcast_select_fusion.3), calls=%async_computation | async-start | bytes 32768 | tf_op jit(solution)/shard_map/all_to_all | solution.py:107
  32.2 10.7 %all-to-all-start.1 = ((bf16[8,2,1536]{2,1,0:T(2,128)(2,1)}), bf16[8,2,1536]{2,1,0:T(2,128)(2,1)S(1)}, u32[]{:S(2)}, u32[]{:S(2)}) async-start(bf16[8,2,1536]{2,1,0:T(2,128)(2,1)} %reshape.277), calls=%async_computation.1 | async-start | bytes 98304 | tf_op jit(solution)/shard_map/all_to_all | solution.py:108
  36.1 46.6 %all-gather.7.cloned.1.call-start = ((), (), s32[]{:S(2)}) async-start(), calls=%async_computation.3 | async-start | bytes 2621440 | tf_op jit(solution)/shard_map/all_gather | solution.py:128
  52.8 3.1 %copy-start.8 = (f32[1024]{0:T(1024)S(1)}, f32[1024]{0:T(1024)}, u32[]{:S(2)}) copy-start(f32[1024]{0:T(1024)} %param.11) | copy-start | bytes 12292
  52.8 3.1 %copy-start.3 = (bf16[64,3,1024]{2,0,1:T(8,128)(2,1)S(1)}, bf16[64,3,1024]{2,0,1:T(8,128)(2,1)}, u32[]{:S(2)}) copy-start(bf16[64,3,1024]{2,0,1:T(8,128)(2,1)} %param.9) | copy-start | bytes 1179652
  55.8 97.2 %all-reduce.2.cloned.1.call-start = ((), (), s32[]{:S(2)}) async-start(), calls=%async_computation.4 | async-start | bytes 131072 | tf_op jit(solution)/shard_map/psum | solution.py:136
  79.1 2.9 %copy-start.1 = (bf16[256,3,1024]{2,0,1:T(8,128)(2,1)S(1)}, bf16[256,3,1024]{2,0,1:T(8,128)(2,1)}, u32[]{:S(2)}) copy-start(bf16[256,3,1024]{2,0,1:T(8,128)(2,1)} %all-gather.5.cloned.1.call-done) | copy-start | bytes 4718596
  82.7 2.6 %copy-start.4 = (bf16[256,1024]{0,1:T(8,128)(2,1)S(1)}, bf16[256,1024]{0,1:T(8,128)(2,1)}, u32[]{:S(2)}) copy-start(bf16[256,1024]{0,1:T(8,128)(2,1)} %copy.65) | copy-start | bytes 1572868
  82.7 2.6 %copy-start.5 = (bf16[3,8,8,1024]{3,2,0,1:T(8,128)(2,1)S(1)}, bf16[3,8,8,1024]{3,2,0,1:T(8,128)(2,1)}, u32[]{:S(2)}) copy-start(bf16[3,8,8,1024]{3,2,0,1:T(8,128)(2,1)} %copy.81) | copy-start | bytes 1179652
  82.7 2.6 %copy-start.7 = (bf16[64,1024]{1,0:T(8,128)(2,1)S(1)}, bf16[64,1024]{1,0:T(8,128)(2,1)}, u32[]{:S(2)}) copy-start(bf16[64,1024]{1,0:T(8,128)(2,1)} %multiply_convert_fusion.2) | copy-start | bytes 393220
Sparse Core Ops, SparseCore 0:
  9.6 22.3 all-gather.4
  55.9 23.1 all-gather.6
  86.5 66.4 all-reduce.1
